TPU v7x, 128 devices: a whole 4x4x4 slice. The times are simulated.
128 devices in a mesh: head: 4 (over x_lo, core), blk: 32 (over x_hi, z, y).
Axes of the slice: x: 4 (x_hi: 2, x_lo: 2; x = x_hi * 2 + x_lo), y: 4, z: 4, core: 2. Of those that a mesh axis runs over, the one named last changes fastest.
Arguments:
- query: bfloat16 [16384, 32, 128], P(('blk', 'head')), may hold values from -12 to 12
- keys: bfloat16 [16384, 4, 128], P(('blk', 'head')), may hold values from -12 to 12
- values: bfloat16 [16384, 4, 128], P(('blk', 'head')), may hold values from -6 to 6
- output: bfloat16 [16384, 32, 128], P(('blk', 'head')), may hold values from -1.5 to 1.5
- dout: bfloat16 [16384, 32, 128], P(('blk', 'head')), may hold values from -192 to 192
Outputs:
- dquery: bfloat16 [16384, 32, 128], P(('blk', 'head'))
- dkeys: bfloat16 [16384, 4, 128], P(('blk', 'head'))
- dvalues: bfloat16 [16384, 4, 128], P(('blk', 'head'))
All inputs are finite; a program needn't handle non-finite values.
Results may differ from a plain program's by a relative error of at most 0.01.
Values may be sent and summed in bfloat16 or wider, within the bound.
A program may use at most 192 MiB of HBM per device.

v0:
```python
import functools
import math

import jax
import jax.numpy as jnp
from jax import lax
from jax.experimental import pallas as pl
from jax.experimental.pallas import tpu as pltpu
from jax.sharding import PartitionSpec as P

BF = jnp.bfloat16
F32 = jnp.float32
MINOR = (((1,), (1,)), ((), ()))
MESH = pl.DeviceIdType.MESH
ANY = pl.BlockSpec(memory_space=pl.ANY)
VMEM = pl.BlockSpec(memory_space=pltpu.VMEM)


class Dims:
    def __init__(self, query, keys, mesh):
        self.tokens, self.q_heads, self.width = query.shape
        self.kv_heads = keys.shape[1]
        self.n_head = mesh.shape["head"]
        self.n_blk = mesh.shape["blk"]
        self.reach = self.n_blk // 8
        self.slots = 2 * self.reach + 1
        self.block = self.tokens * self.n_head
        self.group = self.q_heads // self.n_head
        self.chunk = self.tokens * self.group
        self.rows = self.chunk * self.n_head
        self.scaling = self.width ** (-0.5)
        self.log2_scaling = self.scaling * math.log2(math.e)
        self.score_tile = 512
        self.grad_tile = 256


def aligned(index, size):
    return pl.ds(pl.multiple_of(index * size, size), size)


def remote(src, dst, send, recv, head=None, blk=None):
    where = {}
    if head is not None:
        where["head"] = head
    if blk is not None:
        where["blk"] = blk
    return pltpu.make_async_remote_copy(
        src_ref=src, dst_ref=dst, send_sem=send, recv_sem=recv, device_id=where, device_id_type=MESH
    )


def split_heads(dm, source, staged, wide, part):
    wide[...] = source[...].astype(F32)
    for g in range(dm.n_head):
        staged[g, part] = wide[pl.ds(g, dm.tokens, stride=dm.kv_heads), :].astype(BF)


def delta_rows(dm, dout, output, rows):
    ones = jnp.ones((8, dm.width), BF)
    for g in range(dm.n_head):
        heads = slice(g * dm.group, (g + 1) * dm.group)
        product = dout[:, heads, :].astype(F32) * output[:, heads, :].astype(F32)
        product = product.reshape(dm.chunk, dm.width)
        high = product.astype(BF)
        low = (product - high.astype(F32)).astype(BF)
        total = lax.dot_general(ones, high, MINOR, preferred_element_type=F32) + lax.dot_general(
            ones, low, MINOR, preferred_element_type=F32
        )
        rows[g] = total[0:1, :].astype(BF).astype(F32)


def score_phase(dm, keys, q_t, probs, scores, tops, sums, b, first, count):
    block, tile = dm.block, dm.score_tile
    for i in range(count + 1):
        if i < count:
            columns = aligned(first + i, tile)
            scores[i % 2] = jnp.dot(keys, q_t[:, columns], preferred_element_type=F32)
        if i > 0:
            columns = aligned(first + i - 1, tile)
            x = scores[(i - 1) % 2]
            top = jnp.max(jnp.max(x.reshape(block // 8, 8, tile), axis=0), axis=0, keepdims=True)
            p = jnp.exp2((x - top) * dm.log2_scaling)
            total = jnp.sum(jnp.sum(p.reshape(block // 8, 8, tile), axis=0), axis=0, keepdims=True)
            probs[aligned(b, block), columns] = p.astype(BF)
            tops[pl.ds(b, 1), columns] = top
            sums[pl.ds(b, 1), columns] = total


def combine(dm, tops, sums, factors):
    top = tops[...]
    weight = jnp.exp2((top - jnp.max(top, axis=0, keepdims=True)) * dm.log2_scaling)
    factors[...] = weight / jnp.sum(weight * sums[...], axis=0, keepdims=True)


def gradient_phase(dm, keys_t, values, q_t, do_t, delta, probs, factors, dq_t, small, b):
    block, tile = dm.block, dm.grad_tile
    count = dm.rows // tile
    per_chunk = dm.chunk // tile
    rows = aligned(b, block)
    dk = jnp.zeros((dm.width, block), F32)
    dv = jnp.zeros((dm.width, block), F32)
    for i in range(count + 1):
        if i < count:
            columns = slice(i * tile, (i + 1) * tile)
            inner = slice((i % per_chunk) * tile, (i % per_chunk + 1) * tile)
            prob_grad = jnp.dot(values, do_t[:, columns], preferred_element_type=F32)
            grad = probs[rows, columns].astype(F32) * (prob_grad - delta[i // per_chunk, :, inner])
            small[i % 2] = grad.astype(BF)
        if i > 0:
            columns = slice((i - 1) * tile, i * tile)
            factor = factors[pl.ds(b, 1), columns]
            scaled = factor * dm.scaling
            grad = small[(i - 1) % 2]
            do_scaled = (do_t[:, columns].astype(F32) * factor).astype(BF)
            q_scaled = (q_t[:, columns].astype(F32) * scaled).astype(BF)
            dv = dv + lax.dot_general(do_scaled, probs[rows, columns], MINOR, preferred_element_type=F32)
            dk = dk + lax.dot_general(q_scaled, grad, MINOR, preferred_element_type=F32)
            dq_t[:, columns] += jnp.dot(keys_t, grad, preferred_element_type=F32) * scaled
    return dk, dv


def kernel(dm, query, dout, output, keys, values, dquery, dkeys, dvalues,
           staged, wide, drow, dout_v, output_v, q_in, do_in, delta, kv,
           keys_t, q_t, do_t, probs, scores, small, tops, sums, factors, dq_t,
           dkv, inbox, relay, upright, total, heads, landed, dq,
           local, s_kv, r_kv, s_q, r_q, s_do, r_do, s_de, r_de, s_near, s_far, s_pass, r_n,
           s_in, r_in, s_up, r_up, s_dq, r_dq, s_h, r_h):
    me = lax.axis_index("head")
    position = lax.axis_index("blk")
    n, w = dm.n_head, dm.reach
    place = lax.rem(position, w)
    pair = me // 2
    core = lax.rem(me, 2)
    mate = pair * 2 + 1 - core
    across = [(1 - pair) * 2 + core, (1 - pair) * 2 + 1 - core]
    peers = across + [mate]
    has_before = position - w >= 0
    has_after = position + w < dm.n_blk
    others = [lax.rem(place + s, w) for s in range(1, w)]

    own = [
        pltpu.make_async_copy(dout, dout_v, local.at[0]),
        pltpu.make_async_copy(output, output_v, local.at[1]),
        pltpu.make_async_copy(query.at[:, aligned(me, dm.group), :], q_in.at[me], local.at[2]),
        pltpu.make_async_copy(dout.at[:, aligned(me, dm.group), :], do_in.at[me], local.at[3]),
    ]
    for copy in own:
        copy.start()
    barrier = pltpu.get_barrier_semaphore()
    for g in peers:
        pl.semaphore_signal(barrier, inc=1, device_id={"head": g}, device_id_type=MESH)
    for c in others:
        pl.semaphore_signal(barrier, inc=1, device_id={"blk": position + c - place}, device_id_type=MESH)

    @pl.when(has_before)
    def _():
        pl.semaphore_signal(barrier, inc=1, device_id={"blk": position - w}, device_id_type=MESH)

    @pl.when(has_after)
    def _():
        pl.semaphore_signal(barrier, inc=1, device_id={"blk": position + w}, device_id_type=MESH)

    split_heads(dm, keys, staged, wide, 0)
    split_heads(dm, values, staged, wide, 1)
    groups = position // w
    ends = jnp.minimum(groups, 1) + jnp.minimum(dm.n_blk // w - 1 - groups, 1)
    pl.semaphore_wait(barrier, n - 1 + w - 1 + ends)

    def kv_copy(g, source, to):
        return remote(staged.at[g], kv.at[w, :, aligned(source, dm.tokens), :], s_kv.at[g], r_kv.at[source], head=to)

    def q_copy(g, source, to):
        return remote(query.at[:, aligned(g, dm.group), :], q_in.at[source], s_q.at[g], r_q.at[source], head=to)

    def do_copy(g, source, to):
        return remote(dout.at[:, aligned(g, dm.group), :], do_in.at[source], s_do.at[g], r_do.at[source], head=to)

    def de_copy(g, source, to):
        return remote(drow.at[g], delta.at[source], s_de.at[g], r_de.at[source], head=to)

    for make in (kv_copy, q_copy):
        for g in peers:
            make(g, me, g).start()
    kv_own = pltpu.make_async_copy(staged.at[me], kv.at[w, :, aligned(me, dm.tokens), :], local.at[4])
    kv_own.start()
    own[0].wait()
    own[1].wait()
    delta_rows(dm, dout_v, output_v, drow)
    for g in peers:
        de_copy(g, me, g).start()
    de_own = pltpu.make_async_copy(drow.at[me], delta.at[me], local.at[5])
    de_own.start()
    kv_own.wait()
    for g in peers:
        kv_copy(me, g, g).wait_recv()

    def near(c):
        return remote(kv.at[w], kv.at[w + place - c], s_near.at[c], r_n.at[w + place - c], blk=position + c - place)

    def far(step, side):
        slot = w - step
        return remote(kv.at[w], kv.at[slot], s_far.at[side], r_n.at[slot], blk=position + step)

    def passed(c, source):
        slot = lax.rem(place - c + 2 * w, 2 * w)
        return remote(kv.at[source], kv.at[slot], s_pass.at[c], r_n.at[slot], blk=position + c - place)

    @pl.when(has_before)
    def _():
        far(-w, 0).start()

    @pl.when(has_after)
    def _():
        far(w, 1).start()

    for c in others:
        near(c).start()

    for at in range(0, dm.rows, 512):
        dq_t[:, at:at + 512] = jnp.zeros((dm.width, 512), F32)
    tops[...] = jnp.full((dm.slots, dm.rows), -jnp.inf, F32)
    sums[...] = jnp.zeros((dm.slots, dm.rows), F32)

    def turn(source, target, g):
        target[:, aligned(g, dm.chunk)] = source[g].astype(F32).reshape(dm.chunk, dm.width).T.astype(BF)

    own[2].wait()
    turn(q_in, q_t, me)
    q_copy(me, mate, mate).wait_recv()
    turn(q_in, q_t, mate)

    def exists(slot):
        other = position - w + slot
        return (other >= 0) & (other < dm.n_blk)

    def arrival(j):
        kind, s = j // (w - 1), lax.rem(j, w - 1) + 1
        apart = lax.rem(place + s, w) - place
        side = lax.rem(w * s, 3 * w)
        inner = lax.rem(w * (2 - kind) + apart + 2 * w, 2 * w)
        return jnp.where(kind == 0, side, inner)

    half = dm.rows // 2 // dm.score_tile

    @pl.loop(0, dm.slots)
    def _(j):
        slot = arrival(j)

        @pl.when(exists(slot))
        def _():
            @pl.when(j > 0)
            def _():
                remote(kv.at[w], kv.at[slot], s_far.at[0], r_n.at[slot], head=mate).wait_recv()

            @pl.when((j == 1) & has_after)
            def _():
                for c in range(w):
                    @pl.when(c > place)
                    def _():
                        passed(c, 2 * w).start()

            @pl.when((j == 2) & has_before)
            def _():
                for c in range(w):
                    @pl.when(c < place)
                    def _():
                        passed(c, 0).start()

            keys_t[:, aligned(slot, dm.block)] = kv[slot, 0].T
            score_phase(dm, kv[slot, 0], q_t, probs, scores, tops, sums, slot, pair * half, half)

        @pl.when(j == 4)
        def _():
            for g in peers:
                do_copy(g, me, g).start()

    for g in across:
        q_copy(me, g, g).wait_recv()
        turn(q_in, q_t, g)

    @pl.loop(0, dm.slots)
    def _(slot):
        @pl.when(exists(slot))
        def _():
            score_phase(dm, kv[slot, 0], q_t, probs, scores, tops, sums, slot, (1 - pair) * half, half)

    combine(dm, tops, sums, factors)
    own[3].wait()
    turn(do_in, do_t, me)
    de_own.wait()
    for g in [mate] + across:
        do_copy(me, g, g).wait_recv()
        de_copy(me, g, g).wait_recv()
        turn(do_in, do_t, g)

    def to_member(direct, c):
        apart = c - place
        slot = w + apart if direct else lax.rem(apart + 2 * w, 2 * w)
        box = w * direct
        return remote(dkv.at[slot], inbox.at[box + place], s_in.at[box + c], r_in.at[box + place], blk=position + apart)

    def from_member(direct, c):
        box = w * direct
        return remote(dkv.at[w], inbox.at[box + c], s_in.at[box + c], r_in.at[box + c], blk=position + c - place)

    def to_side(side):
        step = w if side else -w
        return remote(relay.at[side], upright.at[1 - side], s_up.at[side], r_up.at[1 - side], blk=position + step)

    def from_side(side):
        step = w if side else -w
        return remote(relay.at[side], upright.at[side], s_up.at[side], r_up.at[side], blk=position + step)

    def gather_side(side):
        relay_sum = dkv[2 * w * side].astype(F32)
        total[...] = relay_sum
        for c in range(w):
            member = (c > place) if side else (c < place)

            @pl.when(member)
            def _():
                from_member(0, c).wait_recv()
                total[...] += inbox[c].astype(F32)

        relay[side] = total[...].astype(BF)
        to_side(side).start()

    def departure(j):
        s = jnp.where(j < w - 1, j + 1, j - w)
        apart = lax.rem(place + s, w) - place
        return jnp.where(
            j < w - 1,
            lax.rem(apart + 2 * w, 2 * w),
            jnp.where(j < w + 1, (j - w + 1) * 2 * w, jnp.where(j < 2 * w, w + apart, w)),
        )

    @pl.loop(0, dm.slots)
    def _(j):
        slot = departure(j)

        @pl.when(exists(slot))
        def _():
            dk, dv = gradient_phase(
                dm, keys_t[:, aligned(slot, dm.block)], kv[slot, 1], q_t, do_t, delta, probs, factors, dq_t, small, slot
            )
            dkv[slot, 0] = dk.astype(BF)
            dkv[slot, 1] = dv.astype(BF)

            @pl.when(j < w - 1)
            def _():
                to_member(0, lax.rem(place + j + 1, w)).start()

            @pl.when((j > w) & (j < 2 * w))
            def _():
                to_member(1, lax.rem(place + j - w + 2 * w, w)).start()

        @pl.when((j == w + 1) & has_before)
        def _():
            gather_side(0)

        @pl.when((j == w + 2) & has_after)
        def _():
            gather_side(1)

    def dq_copy(g, source, to):
        return remote(dq.at[g], dquery.at[:, aligned(source, dm.group), :], s_dq.at[g], r_dq.at[source], head=to)

    for g in peers + [me]:
        dq[g] = dq_t[:, aligned(g, dm.chunk)].T.reshape(dm.tokens, dm.group, dm.width).astype(BF)
        if g is not me:
            dq_copy(g, me, g).start()
    dq_own = pltpu.make_async_copy(dq.at[me], dquery.at[:, aligned(me, dm.group), :], local.at[6])
    dq_own.start()

    total[...] = dkv[w].astype(F32)
    for c in others:
        from_member(1, c).wait_recv()
        total[...] += inbox[w + c].astype(F32)

    @pl.when(has_before)
    def _():
        from_side(0).wait_recv()
        total[...] += upright[0].astype(F32)

    @pl.when(has_after)
    def _():
        from_side(1).wait_recv()
        total[...] += upright[1].astype(F32)

    for part in range(2):
        rows = total[part].T.astype(BF)
        for g in range(n):
            heads[g, part] = rows[g * dm.tokens:(g + 1) * dm.tokens, :]

    def head_copy(g, source, to):
        return remote(heads.at[g], landed.at[source], s_h.at[g], r_h.at[source], head=to)

    for g in peers:
        head_copy(g, me, g).start()
    head_own = pltpu.make_async_copy(heads.at[me], landed.at[me], local.at[7])
    head_own.start()
    head_own.wait()
    for g in peers:
        head_copy(me, g, g).wait_recv()
    for part, out in ((0, dkeys), (1, dvalues)):
        for g in range(n):
            wide[pl.ds(g, dm.tokens, stride=dm.kv_heads), :] = landed[g, part].astype(F32)
        out[...] = wide[...].astype(BF)

    dq_own.wait()
    for g in peers:
        for make in (kv_copy, q_copy, do_copy, de_copy, dq_copy, head_copy):
            make(g, me, g).wait_send()
        dq_copy(me, g, g).wait_recv()
    for c in others:
        near(c).wait_send()
        to_member(1, c).wait_send()

    @pl.when(has_before)
    def _():
        far(-w, 0).wait_send()
        to_side(0).wait_send()

    @pl.when(has_after)
    def _():
        far(w, 1).wait_send()
        to_side(1).wait_send()

    for c in range(w):

        @pl.when(has_before & (c < place))
        def _():
            passed(c, 0).wait_send()

        @pl.when(has_after & (c > place))
        def _():
            passed(c, 2 * w).wait_send()

        @pl.when(has_after & (c < place))
        def _():
            to_member(0, c).wait_send()

        @pl.when(has_before & (c > place))
        def _():
            to_member(0, c).wait_send()


def fused(dm, query, keys, values, output, dout):
    n, w, dma = dm.n_head, dm.reach, pltpu.SemaphoreType.DMA
    flat = dm.tokens * dm.kv_heads
    span = dm.slots * dm.block
    chunked = (n, dm.tokens, dm.group, dm.width)
    terms = (2, dm.width, dm.block)
    return pl.pallas_call(
        functools.partial(kernel, dm),
        out_shape=(
            jax.ShapeDtypeStruct(query.shape, BF),
            jax.ShapeDtypeStruct((flat, dm.width), BF),
            jax.ShapeDtypeStruct((flat, dm.width), BF),
        ),
        in_specs=[ANY, ANY, ANY, VMEM, VMEM],
        out_specs=[ANY, VMEM, VMEM],
        scratch_shapes=[
            pltpu.VMEM((n, 2, dm.tokens, dm.width), BF),
            pltpu.VMEM((flat, dm.width), F32),
            pltpu.VMEM((n, 1, dm.chunk), F32),
            pltpu.VMEM(query.shape, BF),
            pltpu.VMEM(query.shape, BF),
            pltpu.VMEM(chunked, BF),
            pltpu.VMEM(chunked, BF),
            pltpu.VMEM((n, 1, dm.chunk), F32),
            pltpu.VMEM((dm.slots, 2, dm.block, dm.width), BF),
            pltpu.VMEM((dm.width, span), BF),
            pltpu.VMEM((dm.width, dm.rows), BF),
            pltpu.VMEM((dm.width, dm.rows), BF),
            pltpu.VMEM((span, dm.rows), BF),
            pltpu.VMEM((2, dm.block, dm.score_tile), F32),
            pltpu.VMEM((2, dm.block, dm.grad_tile), BF),
            pltpu.VMEM((dm.slots, dm.rows), F32),
            pltpu.VMEM((dm.slots, dm.rows), F32),
            pltpu.VMEM((dm.slots, dm.rows), F32),
            pltpu.VMEM((dm.width, dm.rows), F32),
            pltpu.VMEM((dm.slots,) + terms, BF),
            pltpu.VMEM((2 * w,) + terms, BF),
            pltpu.VMEM((2,) + terms, BF),
            pltpu.VMEM((2,) + terms, BF),
            pltpu.VMEM(terms, F32),
            pltpu.VMEM((n, 2, dm.tokens, dm.width), BF),
            pltpu.VMEM((n, 2, dm.tokens, dm.width), BF),
            pltpu.VMEM(chunked, BF),
            dma((8,)),
        ]
        + [dma((n,))] * 8
        + [dma((w,)), dma((2,)), dma((w,)), dma((dm.slots,))]
        + [dma((2 * w,)), dma((2 * w,)), dma((2,)), dma((2,))]
        + [dma((n,))] * 4,
        compiler_params=pltpu.CompilerParams(
            collective_id=0, has_side_effects=True, vmem_limit_bytes=63 * 2**20
        ),
        name="banded_attention_gradients",
    )(
        query,
        dout,
        output,
        keys.reshape(flat, dm.width),
        values.reshape(flat, dm.width),
    )


def solution(mesh):
    def on_device(query, keys, values, output, dout):
        dm = Dims(query, keys, mesh)
        dquery, dkeys, dvalues = fused(dm, query, keys, values, output, dout)
        return dquery, dkeys.reshape(keys.shape), dvalues.reshape(values.shape)

    spec = P(("blk", "head"), None, None)
    return jax.shard_map(
        on_device, mesh=mesh, in_specs=(spec,) * 5, out_specs=(spec,) * 3, check_vma=False
    )
```

profile of v0, /device:TPU:105, one launch (start us, length us, event | category | flops | bytes accessed | tf_op | source)
XLA Modules:
  0.0 119.1 jit_solution(10846622604543431079)
XLA Ops:
  0.6 114.5 %banded_attention_gradients.1 = (bf16[128,32,128]{2,1,0:T(8,128)(2,1)}, bf16[512,128]{1,0:T(8,128)(2,1)}, bf16[512,128]{1,0:T(8,128)(2,1)}) custom-call(bf16[128,32,128]{2,1,0:T(8,128)(2,1)} %query.1, bf16[128,32,128]{2,1,0:T(8,128)(2,1)} %dout.1, bf16[128,32,128]{2,1,0:T(8,128)(2,1)} %output.1, bf16[512,128]{1,0:T(8,128)(2,1)} %bitcast.6, ...), custom_call_target="tpu_custom_call" | custom-call | tf_op jit(solution)/shard_map/banded_attention_gradients/pallas_call | solution.py:454
  115.2 0.0 copy-start.1
  115.2 2.3 %copy.11 = bf16[128,32,128]{2,1,0:T(8,128)(2,1)} copy(bf16[128,32,128]{2,1,0:T(8,128)(2,1)} %get-tuple-element.12) | data formatting | bytes 2097152
  117.5 0.0 copy-done.1
  117.5 0.0 copy-start
  117.5 0.7 copy.12
  118.1 0.3 copy-done
  118.4 0.7 copy.13
Async XLA Ops:
  115.2 2.3 %copy-start.1 = (bf16[512,128]{1,0:T(8,128)(2,1)S(1)}, bf16[512,128]{1,0:T(8,128)(2,1)}, u32[]{:S(2)}) copy-start(bf16[512,128]{1,0:T(8,128)(2,1)} %get-tuple-element.7) | copy-start | bytes 393220
  117.5 1.0 copy-start
where the time goes:
time: 119 us
  Pallas kernels  115 us (97%)
  local copies, waits for them, and re-layouts  3.91 us (3%)
    pallas_call x1, Pallas kernels, fused(): pl.pallas_call(functools.partial(kernel, dm), out_shape=(jax.ShapeDtypeSt...  115 us
    unnamed x7, local copies, waits for them, and re-layouts  3.91 us

commit v1 on v0

v1 whole, which is shorter than its diff:
```python
import functools
import math

import jax
import jax.numpy as jnp
from jax import lax
from jax.experimental import pallas as pl
from jax.experimental.pallas import tpu as pltpu
from jax.sharding import PartitionSpec as P

BF = jnp.bfloat16
F32 = jnp.float32
MINOR = (((1,), (1,)), ((), ()))
MESH = pl.DeviceIdType.MESH
ANY = pl.BlockSpec(memory_space=pl.ANY)
VMEM = pl.BlockSpec(memory_space=pltpu.VMEM)


class Dims:
    def __init__(self, query, keys, mesh):
        self.tokens, self.q_heads, self.width = query.shape
        self.kv_heads = keys.shape[1]
        self.n_head = mesh.shape["head"]
        self.n_blk = mesh.shape["blk"]
        self.reach = self.n_blk // 8
        self.slots = 2 * self.reach + 1
        self.block = self.tokens * self.n_head
        self.group = self.q_heads // self.n_head
        self.chunk = self.tokens * self.group
        self.rows = self.chunk * self.n_head
        self.scaling = self.width ** (-0.5)
        self.log2_scaling = self.scaling * math.log2(math.e)
        self.score_tile = 512
        self.grad_tile = 256


def aligned(index, size):
    return pl.ds(pl.multiple_of(index * size, size), size)


def remote(src, dst, send, recv, head=None, blk=None):
    where = {}
    if head is not None:
        where["head"] = head
    if blk is not None:
        where["blk"] = blk
    return pltpu.make_async_remote_copy(
        src_ref=src, dst_ref=dst, send_sem=send, recv_sem=recv, device_id=where, device_id_type=MESH
    )


def split_heads(dm, source, staged, wide, part):
    wide[...] = source[...].astype(F32)
    for g in range(dm.n_head):
        staged[g, part] = wide[pl.ds(g, dm.tokens, stride=dm.kv_heads), :].astype(BF)


def delta_rows(dm, dout, output, rows):
    ones = jnp.ones((8, dm.width), BF)
    for g in range(dm.n_head):
        heads = slice(g * dm.group, (g + 1) * dm.group)
        product = dout[:, heads, :].astype(F32) * output[:, heads, :].astype(F32)
        product = product.reshape(dm.chunk, dm.width)
        high = product.astype(BF)
        low = (product - high.astype(F32)).astype(BF)
        total = lax.dot_general(ones, high, MINOR, preferred_element_type=F32) + lax.dot_general(
            ones, low, MINOR, preferred_element_type=F32
        )
        rows[g] = total[0:1, :].astype(BF).astype(F32)


def score_phase(dm, keys, q_t, probs, scores, tops, sums, b, chunk, count):
    block, tile = dm.block, dm.score_tile
    count = count * dm.chunk // tile
    start = chunk * (dm.chunk // tile)
    for i in range(count + 1):
        if i < count:
            columns = aligned(start + i, tile)
            scores[i % 2] = jnp.dot(keys, q_t[:, columns], preferred_element_type=F32)
        if i > 0:
            columns = aligned(start + i - 1, tile)
            x = scores[(i - 1) % 2]
            top = jnp.max(jnp.max(x.reshape(block // 8, 8, tile), axis=0), axis=0, keepdims=True)
            p = jnp.exp2((x - top) * dm.log2_scaling)
            total = jnp.sum(jnp.sum(p.reshape(block // 8, 8, tile), axis=0), axis=0, keepdims=True)
            probs[aligned(b, block), columns] = p.astype(BF)
            tops[pl.ds(b, 1), columns] = top
            sums[pl.ds(b, 1), columns] = total


def combine(dm, tops, sums, factors):
    top = tops[...]
    weight = jnp.exp2((top - jnp.max(top, axis=0, keepdims=True)) * dm.log2_scaling)
    factors[...] = weight / jnp.sum(weight * sums[...], axis=0, keepdims=True)


def gradient_phase(dm, keys_t, values, q_t, do_t, delta, probs, factors, dq_t, small, b, chunk, count):
    block, tile = dm.block, dm.grad_tile
    per_chunk = dm.chunk // tile
    count = count * per_chunk
    start = chunk * per_chunk
    rows = aligned(b, block)
    dk = jnp.zeros((dm.width, block), F32)
    dv = jnp.zeros((dm.width, block), F32)
    for i in range(count + 1):
        if i < count:
            columns = aligned(start + i, tile)
            inner = slice((i % per_chunk) * tile, (i % per_chunk + 1) * tile)
            prob_grad = jnp.dot(values, do_t[:, columns], preferred_element_type=F32)
            grad = probs[rows, columns].astype(F32) * (prob_grad - delta[chunk + i // per_chunk, :, inner])
            small[i % 2] = grad.astype(BF)
        if i > 0:
            columns = aligned(start + i - 1, tile)
            factor = factors[pl.ds(b, 1), columns]
            scaled = factor * dm.scaling
            grad = small[(i - 1) % 2]
            do_scaled = (do_t[:, columns].astype(F32) * factor).astype(BF)
            q_scaled = (q_t[:, columns].astype(F32) * scaled).astype(BF)
            dv = dv + lax.dot_general(do_scaled, probs[rows, columns], MINOR, preferred_element_type=F32)
            dk = dk + lax.dot_general(q_scaled, grad, MINOR, preferred_element_type=F32)
            dq_t[:, columns] += jnp.dot(keys_t, grad, preferred_element_type=F32) * scaled
    return dk, dv


def pick(index, choices):
    value = choices[-1]
    for at in range(len(choices) - 2, -1, -1):
        value = jnp.where(index == at, choices[at], value)
    return value


def kernel(dm, query, dout, output, keys, values, dquery, dkeys, dvalues,
           keys_v, values_v, staged, wide, drow, dout_v, output_v, q_in, do_in, delta, kv,
           keys_t, q_t, do_t, probs, scores, small, tops, sums, factors, dq_t,
           dkv, inbox, total, heads, landed, dq,
           local, s_kv, r_kv, s_q, r_q, s_do, r_do, s_de, r_de, s_dq, r_dq, s_h, r_h,
           s_own, s_rel, r_n, s_out, r_box):
    me = lax.axis_index("head")
    position = lax.axis_index("blk")
    n, w = dm.n_head, dm.reach
    pair = me // 2
    core = lax.rem(me, 2)
    mate = pair * 2 + 1 - core
    across = [(1 - pair) * 2 + core, (1 - pair) * 2 + 1 - core]
    peers = [mate] + across
    place = lax.rem(position, w)
    a = place + 1 - 2 * lax.rem(place, 2)
    b = w - 1 - place
    o = lax.rem(place + 2, w)
    has_before = position - w >= 0
    has_after = position + w < dm.n_blk
    base = position - place

    def same(d):
        return w + d - place

    def side(d):
        return lax.rem(d - place + 2 * w, 2 * w)

    def exists(slot):
        other = position - w + slot
        return (other >= 0) & (other < dm.n_blk)

    own = [
        pltpu.make_async_copy(keys, keys_v, local.at[0]),
        pltpu.make_async_copy(values, values_v, local.at[1]),
        pltpu.make_async_copy(dout, dout_v, local.at[2]),
        pltpu.make_async_copy(output, output_v, local.at[3]),
        pltpu.make_async_copy(query.at[:, aligned(me, dm.group), :], q_in.at[me], local.at[4]),
        pltpu.make_async_copy(dout.at[:, aligned(me, dm.group), :], do_in.at[me], local.at[5]),
    ]
    for copy in own:
        copy.start()
    barrier = pltpu.get_barrier_semaphore()
    for g in peers:
        pl.semaphore_signal(barrier, inc=1, device_id={"head": g}, device_id_type=MESH)
    for c in (a, b):
        pl.semaphore_signal(barrier, inc=1, device_id={"blk": base + c}, device_id_type=MESH)

    @pl.when(has_before)
    def _():
        pl.semaphore_signal(barrier, inc=1, device_id={"blk": position - w}, device_id_type=MESH)

    @pl.when(has_after)
    def _():
        pl.semaphore_signal(barrier, inc=1, device_id={"blk": position + w}, device_id_type=MESH)

    own[0].wait()
    split_heads(dm, keys_v, staged, wide, 0)
    own[1].wait()
    split_heads(dm, values_v, staged, wide, 1)
    groups = position // w
    ends = jnp.minimum(groups, 1) + jnp.minimum(dm.n_blk // w - 1 - groups, 1)
    pl.semaphore_wait(barrier, n - 1 + 2 + ends)

    def kv_copy(g, source, to):
        return remote(staged.at[g], kv.at[w, :, aligned(source, dm.tokens), :], s_kv.at[g], r_kv.at[source], head=to)

    def q_copy(g, source, to):
        return remote(query.at[:, aligned(g, dm.group), :], q_in.at[source], s_q.at[g], r_q.at[source], head=to)

    def do_copy(g, source, to):
        return remote(dout.at[:, aligned(g, dm.group), :], do_in.at[source], s_do.at[g], r_do.at[source], head=to)

    def de_copy(g, source, to):
        return remote(drow.at[g], delta.at[source], s_de.at[g], r_de.at[source], head=to)

    for make in (kv_copy, q_copy):
        for g in peers:
            make(g, me, g).start()
    kv_own = pltpu.make_async_copy(staged.at[me], kv.at[w, :, aligned(me, dm.tokens), :], local.at[6])
    kv_own.start()
    own[4].wait()

    def turn(source, target, g):
        target[:, aligned(g, dm.chunk)] = source[g].astype(F32).reshape(dm.chunk, dm.width).T.astype(BF)

    turn(q_in, q_t, me)
    kv_own.wait()
    for g in peers:
        kv_copy(me, g, g).wait_recv()

    def hop(source, slot, sem, to):
        return remote(kv.at[source], kv.at[slot], sem, r_n.at[slot], blk=to)

    def arrived(slot):
        hop(slot, slot, s_own.at[0], base + a).wait_recv()

    to_a = hop(w, w + place - a, s_own.at[0], base + a)
    to_b = hop(w, w + place - b, s_own.at[1], base + b)
    to_before = hop(w, 2 * w, s_own.at[2], position - w)
    to_after = hop(w, 0, s_own.at[3], position + w)
    on_same = hop(same(a), w + a - b, s_rel.at[0], base + b)
    before_on = [hop(0, place - d, s_rel.at[1 + k], base + d) for k, d in enumerate((a, b))]
    after_on = [hop(2 * w, 2 * w + place - d, s_rel.at[1 + k], base + d) for k, d in enumerate((a, b))]
    on_side = hop(side(b), lax.rem(b - a + 2 * w, 2 * w), s_rel.at[3], base + a)
    to_a.start()
    to_b.start()

    @pl.when(has_before)
    def _():
        to_before.start()

    @pl.when(has_after)
    def _():
        to_after.start()

    own[2].wait()
    own[3].wait()
    delta_rows(dm, dout_v, output_v, drow)
    for g in peers:
        de_copy(g, me, g).start()
    de_own = pltpu.make_async_copy(drow.at[me], delta.at[me], local.at[7])
    de_own.start()
    for at in range(0, dm.rows, 512):
        dq_t[:, at:at + 512] = jnp.zeros((dm.width, 512), F32)
    tops[...] = jnp.full((dm.slots, dm.rows), -jnp.inf, F32)
    sums[...] = jnp.zeros((dm.slots, dm.rows), F32)
    q_copy(me, mate, mate).wait_recv()
    turn(q_in, q_t, mate)

    def early(j):
        return pick(j, [jnp.int32(w), same(a), same(b), jnp.int32(0), jnp.int32(2 * w)])

    def late(j):
        return pick(j, [side(b), same(o), side(a), side(o)])

    @pl.loop(0, w + 1)
    def _(j):
        slot = early(j)

        @pl.when(exists(slot))
        def _():
            @pl.when(j > 0)
            def _():
                arrived(slot)

            @pl.when(j == 1)
            def _():
                on_same.start()

            for k, d in enumerate((a, b)):

                @pl.when((j == 3) & (d < place))
                def _():
                    before_on[k].start()

                @pl.when((j == 4) & (d > place))
                def _():
                    after_on[k].start()

            keys_t[:, aligned(slot, dm.block)] = kv[slot, 0].T
            score_phase(dm, kv[slot, 0], q_t, probs, scores, tops, sums, slot, pair * 2, 2)

    for g in peers:
        do_copy(g, me, g).start()
    for g in across:
        q_copy(me, g, g).wait_recv()
        turn(q_in, q_t, g)

    @pl.loop(0, w + 1)
    def _(j):
        slot = early(j)

        @pl.when(exists(slot))
        def _():
            score_phase(dm, kv[slot, 0], q_t, probs, scores, tops, sums, slot, (1 - pair) * 2, 2)

    own[5].wait()
    turn(do_in, do_t, me)
    de_own.wait()
    do_copy(me, mate, mate).wait_recv()
    turn(do_in, do_t, mate)

    @pl.loop(0, w)
    def _(j):
        slot = late(j)

        @pl.when(exists(slot))
        def _():
            arrived(slot)

            @pl.when(j == 0)
            def _():
                on_side.start()

            keys_t[:, aligned(slot, dm.block)] = kv[slot, 0].T
            score_phase(dm, kv[slot, 0], q_t, probs, scores, tops, sums, slot, 0, 4)

    combine(dm, tops, sums, factors)
    de_copy(me, mate, mate).wait_recv()
    for g in across:
        do_copy(me, g, g).wait_recv()
        de_copy(me, g, g).wait_recv()
        turn(do_in, do_t, g)

    def give(slot, box, k, to):
        return remote(dkv.at[slot], inbox.at[box], s_out.at[k], r_box.at[box], blk=to)

    def taken(box):
        give(w, box, box, base + a).wait_recv()

    def gradients(slot, chunk, count):
        return gradient_phase(
            dm, keys_t[:, aligned(slot, dm.block)], kv[slot, 1], q_t, do_t, delta, probs, factors, dq_t, small,
            slot, chunk, count
        )

    def first(j):
        return pick(j, [side(o), same(o), side(a), side(b), same(b)])

    def last(j):
        return pick(j, [jnp.int32(0), jnp.int32(2 * w), same(a), jnp.int32(w)])

    def add(slot, box):
        taken(box)
        dkv[slot] = (dkv[slot].astype(F32) + inbox[box].astype(F32)).astype(BF)

    @pl.loop(0, w + 1)
    def _(j):
        slot = first(j)

        @pl.when(exists(slot))
        def _():
            dk, dv = gradients(slot, 0, 4)
            dkv[slot, 0] = dk.astype(BF)
            dkv[slot, 1] = dv.astype(BF)

            @pl.when(j == 3)
            def _():
                add(slot, 0)

            give(slot, j, j, base + pick(j, [a, b, a, b, b])).start()

    @pl.loop(0, w)
    def _(j):
        slot = last(j)

        @pl.when(exists(slot))
        def _():
            dk, dv = gradients(slot, (1 - pair) * 2, 2)
            dkv[slot, 0] = dk.astype(BF)
            dkv[slot, 1] = dv.astype(BF)

    def dq_copy(g, source, to):
        return remote(dq.at[g], dquery.at[:, aligned(source, dm.group), :], s_dq.at[g], r_dq.at[source], head=to)

    def turn_back(g):
        dq[g] = dq_t[:, aligned(g, dm.chunk)].T.reshape(dm.tokens, dm.group, dm.width).astype(BF)

    for g in across:
        turn_back(g)
        dq_copy(g, me, g).start()

    @pl.loop(0, w)
    def _(j):
        slot = last(j)

        @pl.when(exists(slot))
        def _():
            dk, dv = gradients(slot, pair * 2, 2)
            dkv[slot, 0] = (dkv[slot, 0].astype(F32) + dk).astype(BF)
            dkv[slot, 1] = (dkv[slot, 1].astype(F32) + dv).astype(BF)

            @pl.when(j == 0)
            def _():
                for box, d in ((2, a), (3, b)):

                    @pl.when(d < place)
                    def _():
                        add(0, box)

                give(0, 7, 6, position - w).start()

            @pl.when(j == 1)
            def _():
                for box, d in ((2, a), (3, b)):

                    @pl.when(d > place)
                    def _():
                        add(2 * w, box)

                give(2 * w, 6, 7, position + w).start()

            @pl.when(j == 2)
            def _():
                add(same(a), 1)
                give(same(a), 5, 5, base + a).start()

    turn_back(mate)
    dq_copy(mate, me, mate).start()
    turn_back(me)
    dq_own = pltpu.make_async_copy(dq.at[me], dquery.at[:, aligned(me, dm.group), :], local.at[8])
    dq_own.start()

    total[...] = dkv[w].astype(F32)
    taken(4)
    total[...] += inbox[4].astype(F32)

    @pl.when(has_before)
    def _():
        taken(6)
        total[...] += inbox[6].astype(F32)

    @pl.when(has_after)
    def _():
        taken(7)
        total[...] += inbox[7].astype(F32)

    taken(5)
    total[...] += inbox[5].astype(F32)
    for part in range(2):
        rows = total[part].T.astype(BF)
        for g in range(n):
            heads[g, part] = rows[g * dm.tokens:(g + 1) * dm.tokens, :]

    def head_copy(g, source, to):
        return remote(heads.at[g], landed.at[source], s_h.at[g], r_h.at[source], head=to)

    for g in peers:
        head_copy(g, me, g).start()
    head_own = pltpu.make_async_copy(heads.at[me], landed.at[me], local.at[9])
    head_own.start()
    head_own.wait()
    for g in peers:
        head_copy(me, g, g).wait_recv()
    for part, out in ((0, dkeys), (1, dvalues)):
        for g in range(n):
            wide[pl.ds(g, dm.tokens, stride=dm.kv_heads), :] = landed[g, part].astype(F32)
        out[...] = wide[...].astype(BF)

    dq_own.wait()
    for g in peers:
        for make in (kv_copy, q_copy, do_copy, de_copy, dq_copy, head_copy):
            make(g, me, g).wait_send()
        dq_copy(me, g, g).wait_recv()
    to_a.wait_send()
    to_b.wait_send()
    on_same.wait_send()

    @pl.when(has_before)
    def _():
        to_before.wait_send()
        give(0, 7, 6, position - w).wait_send()

    @pl.when(has_after)
    def _():
        to_after.wait_send()
        give(2 * w, 6, 7, position + w).wait_send()

    for k, d in enumerate((a, b)):

        @pl.when((d < place) & has_before)
        def _():
            before_on[k].wait_send()

        @pl.when((d > place) & has_after)
        def _():
            after_on[k].wait_send()

    @pl.when(exists(side(b)))
    def _():
        on_side.wait_send()

    for j in range(w + 1):
        slot = [side(o), same(o), side(a), side(b), same(b)][j]

        @pl.when(exists(slot))
        def _():
            give(slot, j, j, base + [a, b, a, b, b][j]).wait_send()

    give(same(a), 5, 5, base + a).wait_send()


def fused(dm, query, keys, values, output, dout):
    n, w, dma = dm.n_head, dm.reach, pltpu.SemaphoreType.DMA
    flat = dm.tokens * dm.kv_heads
    span = dm.slots * dm.block
    chunked = (n, dm.tokens, dm.group, dm.width)
    terms = (2, dm.width, dm.block)
    return pl.pallas_call(
        functools.partial(kernel, dm),
        out_shape=(
            jax.ShapeDtypeStruct(query.shape, BF),
            jax.ShapeDtypeStruct((flat, dm.width), BF),
            jax.ShapeDtypeStruct((flat, dm.width), BF),
        ),
        in_specs=[ANY] * 5,
        out_specs=[ANY, VMEM, VMEM],
        scratch_shapes=[
            pltpu.VMEM((flat, dm.width), BF),
            pltpu.VMEM((flat, dm.width), BF),
            pltpu.VMEM((n, 2, dm.tokens, dm.width), BF),
            pltpu.VMEM((flat, dm.width), F32),
            pltpu.VMEM((n, 1, dm.chunk), F32),
            pltpu.VMEM(query.shape, BF),
            pltpu.VMEM(query.shape, BF),
            pltpu.VMEM(chunked, BF),
            pltpu.VMEM(chunked, BF),
            pltpu.VMEM((n, 1, dm.chunk), F32),
            pltpu.VMEM((dm.slots, 2, dm.block, dm.width), BF),
            pltpu.VMEM((dm.width, span), BF),
            pltpu.VMEM((dm.width, dm.rows), BF),
            pltpu.VMEM((dm.width, dm.rows), BF),
            pltpu.VMEM((span, dm.rows), BF),
            pltpu.VMEM((2, dm.block, dm.score_tile), F32),
            pltpu.VMEM((2, dm.block, dm.grad_tile), BF),
            pltpu.VMEM((dm.slots, dm.rows), F32),
            pltpu.VMEM((dm.slots, dm.rows), F32),
            pltpu.VMEM((dm.slots, dm.rows), F32),
            pltpu.VMEM((dm.width, dm.rows), F32),
            pltpu.VMEM((dm.slots,) + terms, BF),
            pltpu.VMEM((2 * w,) + terms, BF),
            pltpu.VMEM(terms, F32),
            pltpu.VMEM((n, 2, dm.tokens, dm.width), BF),
            pltpu.VMEM((n, 2, dm.tokens, dm.width), BF),
            pltpu.VMEM(chunked, BF),
            dma((10,)),
        ]
        + [dma((n,))] * 12
        + [dma((4,)), dma((4,)), dma((dm.slots,)), dma((8,)), dma((8,))],
        compiler_params=pltpu.CompilerParams(
            collective_id=0, has_side_effects=True, vmem_limit_bytes=63 * 2**20
        ),
        name="banded_attention_gradients",
    )(
        query,
        dout,
        output,
        keys.reshape(flat, dm.width),
        values.reshape(flat, dm.width),
    )


def solution(mesh):
    def on_device(query, keys, values, output, dout):
        dm = Dims(query, keys, mesh)
        dquery, dkeys, dvalues = fused(dm, query, keys, values, output, dout)
        return dquery, dkeys.reshape(keys.shape), dvalues.reshape(values.shape)

    spec = P(("blk", "head"), None, None)
    return jax.shard_map(
        on_device, mesh=mesh, in_specs=(spec,) * 5, out_specs=(spec,) * 3, check_vma=False
    )
```

time: 119 us -> 109 us (0.916)
  the two profiles are of different devices: /device:TPU:105 before, /device:TPU:5 now
where the time goes in v1:
time: 109 us
  Pallas kernels  105 us (96%)
  local copies, waits for them, and re-layouts  3.91 us (4%)
    pallas_call x1, Pallas kernels, fused(): pl.pallas_call(functools.partial(kernel, dm), out_shape=(jax.ShapeDtypeSt...  105 us
    unnamed x7, local copies, waits for them, and re-layouts  3.91 us

profile of v1, /device:TPU:5, one launch (start us, length us, event | category | flops | bytes accessed | tf_op | source)
XLA Modules:
  0.0 109.2 jit_solution(17365015228072807458)
XLA Ops:
  0.6 104.6 %banded_attention_gradients.1 = (bf16[128,32,128]{2,1,0:T(8,128)(2,1)}, bf16[512,128]{1,0:T(8,128)(2,1)}, bf16[512,128]{1,0:T(8,128)(2,1)}) custom-call(bf16[128,32,128]{2,1,0:T(8,128)(2,1)} %query.1, bf16[128,32,128]{2,1,0:T(8,128)(2,1)} %dout.1, bf16[128,32,128]{2,1,0:T(8,128)(2,1)} %output.1, bf16[512,128]{1,0:T(8,128)(2,1)} %bitcast.6, ...), custom_call_target="tpu_custom_call" | custom-call | tf_op jit(solution)/shard_map/banded_attention_gradients/pallas_call | solution.py:521
  105.3 0.0 copy-start.1
  105.3 2.3 %copy.11 = bf16[128,32,128]{2,1,0:T(8,128)(2,1)} copy(bf16[128,32,128]{2,1,0:T(8,128)(2,1)} %get-tuple-element.12) | data formatting | bytes 2097152
  107.6 0.0 copy-done.1
  107.6 0.0 copy-start
  107.6 0.7 copy.12
  108.2 0.3 copy-done
  108.5 0.7 copy.13
Async XLA Ops:
  105.3 2.3 %copy-start.1 = (bf16[512,128]{1,0:T(8,128)(2,1)S(1)}, bf16[512,128]{1,0:T(8,128)(2,1)}, u32[]{:S(2)}) copy-start(bf16[512,128]{1,0:T(8,128)(2,1)} %get-tuple-element.7) | copy-start | bytes 393220
  107.6 1.0 copy-start

commit v2 on v1

--- a/solution.py
+++ b/solution.py
@@ -134,7 +134,7 @@
            keys_t, q_t, do_t, probs, scores, small, tops, sums, factors, dq_t,
            dkv, inbox, total, heads, landed, dq,
            local, s_kv, r_kv, s_q, r_q, s_do, r_do, s_de, r_de, s_dq, r_dq, s_h, r_h,
-           s_own, s_rel, r_n, s_out, r_box):
+           s_hop, r_n, s_out, r_box):
     me = lax.axis_index("head")
     position = lax.axis_index("blk")
     n, w = dm.n_head, dm.reach
@@ -187,14 +187,19 @@
 
     own[0].wait()
     split_heads(dm, keys_v, staged, wide, 0)
-    own[1].wait()
-    split_heads(dm, values_v, staged, wide, 1)
     groups = position // w
     ends = jnp.minimum(groups, 1) + jnp.minimum(dm.n_blk // w - 1 - groups, 1)
     pl.semaphore_wait(barrier, n - 1 + 2 + ends)
 
-    def kv_copy(g, source, to):
-        return remote(staged.at[g], kv.at[w, :, aligned(source, dm.tokens), :], s_kv.at[g], r_kv.at[source], head=to)
+    def part_copy(part, g, source, to):
+        return remote(staged.at[g, part], kv.at[w, part, aligned(source, dm.tokens), :],
+                      s_kv.at[part, g], r_kv.at[part, source], head=to)
+
+    def k_copy(g, source, to):
+        return part_copy(0, g, source, to)
+
+    def v_copy(g, source, to):
+        return part_copy(1, g, source, to)
 
     def q_copy(g, source, to):
         return remote(query.at[:, aligned(g, dm.group), :], q_in.at[source], s_q.at[g], r_q.at[source], head=to)
@@ -205,46 +210,84 @@
     def de_copy(g, source, to):
         return remote(drow.at[g], delta.at[source], s_de.at[g], r_de.at[source], head=to)
 
-    for make in (kv_copy, q_copy):
-        for g in peers:
-            make(g, me, g).start()
-    kv_own = pltpu.make_async_copy(staged.at[me], kv.at[w, :, aligned(me, dm.tokens), :], local.at[6])
-    kv_own.start()
+    for g in peers:
+        k_copy(g, me, g).start()
+    k_own = pltpu.make_async_copy(staged.at[me, 0], kv.at[w, 0, aligned(me, dm.tokens), :], local.at[6])
+    k_own.start()
+    for g in peers:
+        q_copy(g, me, g).start()
+    own[1].wait()
+    split_heads(dm, values_v, staged, wide, 1)
+    for g in peers:
+        v_copy(g, me, g).start()
+    v_own = pltpu.make_async_copy(staged.at[me, 1], kv.at[w, 1, aligned(me, dm.tokens), :], local.at[10])
+    v_own.start()
     own[4].wait()
 
     def turn(source, target, g):
         target[:, aligned(g, dm.chunk)] = source[g].astype(F32).reshape(dm.chunk, dm.width).T.astype(BF)
 
     turn(q_in, q_t, me)
-    kv_own.wait()
-    for g in peers:
-        kv_copy(me, g, g).wait_recv()
-
-    def hop(source, slot, sem, to):
-        return remote(kv.at[source], kv.at[slot], sem, r_n.at[slot], blk=to)
-
-    def arrived(slot):
-        hop(slot, slot, s_own.at[0], base + a).wait_recv()
-
-    to_a = hop(w, w + place - a, s_own.at[0], base + a)
-    to_b = hop(w, w + place - b, s_own.at[1], base + b)
-    to_before = hop(w, 2 * w, s_own.at[2], position - w)
-    to_after = hop(w, 0, s_own.at[3], position + w)
-    on_same = hop(same(a), w + a - b, s_rel.at[0], base + b)
-    before_on = [hop(0, place - d, s_rel.at[1 + k], base + d) for k, d in enumerate((a, b))]
-    after_on = [hop(2 * w, 2 * w + place - d, s_rel.at[1 + k], base + d) for k, d in enumerate((a, b))]
-    on_side = hop(side(b), lax.rem(b - a + 2 * w, 2 * w), s_rel.at[3], base + a)
-    to_a.start()
-    to_b.start()
-
-    @pl.when(has_before)
-    def _():
-        to_before.start()
-
-    @pl.when(has_after)
-    def _():
-        to_after.start()
-
+    k_own.wait()
+    for g in peers:
+        k_copy(me, g, g).wait_recv()
+
+    def hop(part, source, slot, k, to):
+        return remote(kv.at[source, part], kv.at[slot, part], s_hop.at[part, k], r_n.at[part, slot], blk=to)
+
+    def arrived(part, slot):
+        hop(part, slot, slot, 0, base + a).wait_recv()
+
+    def from_own(part, act):
+        act(hop(part, w, w + place - a, 0, base + a))
+        act(hop(part, w, w + place - b, 1, base + b))
+
+        @pl.when(has_before)
+        def _():
+            act(hop(part, w, 2 * w, 2, position - w))
+
+        @pl.when(has_after)
+        def _():
+            act(hop(part, w, 0, 3, position + w))
+
+    def from_first(part, act):
+        for k, d in enumerate((a, b)):
+
+            @pl.when(has_before & (d < place))
+            def _():
+                act(hop(part, 0, place - d, 4 + k, base + d))
+
+            @pl.when(has_after & (d > place))
+            def _():
+                act(hop(part, 2 * w, 2 * w + place - d, 4 + k, base + d))
+
+        act(hop(part, same(a), w + a - b, 6, base + b))
+
+    def from_second(part, act):
+        @pl.when(exists(side(b)))
+        def _():
+            act(hop(part, side(b), lax.rem(b - a + 2 * w, 2 * w), 7, base + a))
+
+    def pass_first(part):
+        @pl.when(has_before)
+        def _():
+            arrived(part, 0)
+
+        @pl.when(has_after)
+        def _():
+            arrived(part, 2 * w)
+
+        arrived(part, same(a))
+        from_first(part, lambda copy: copy.start())
+
+    def pass_second(part):
+        @pl.when(exists(side(b)))
+        def _():
+            arrived(part, side(b))
+
+        from_second(part, lambda copy: copy.start())
+
+    from_own(0, lambda copy: copy.start())
     own[2].wait()
     own[3].wait()
     delta_rows(dm, dout_v, output_v, drow)
@@ -259,80 +302,73 @@
     q_copy(me, mate, mate).wait_recv()
     turn(q_in, q_t, mate)
 
-    def early(j):
-        return pick(j, [jnp.int32(w), same(a), same(b), jnp.int32(0), jnp.int32(2 * w)])
-
-    def late(j):
-        return pick(j, [side(b), same(o), side(a), side(o)])
-
-    @pl.loop(0, w + 1)
+    def order(j):
+        return pick(j, [jnp.int32(w), same(a), same(b), jnp.int32(0), jnp.int32(2 * w),
+                        side(b), side(a), same(o), side(o)])
+
+    @pl.loop(0, dm.slots)
     def _(j):
-        slot = early(j)
+        slot = order(j)
+
+        @pl.when(j == 1)
+        def _():
+            pass_first(0)
+            arrived(0, same(b))
+            v_own.wait()
+            for g in peers:
+                v_copy(me, g, g).wait_recv()
+            from_own(1, lambda copy: copy.start())
+
+        @pl.when(j == 5)
+        def _():
+            pass_second(0)
+            for g in peers:
+                do_copy(g, me, g).start()
+
+        @pl.when(j == 7)
+        def _():
+            pass_first(1)
 
         @pl.when(exists(slot))
         def _():
-            @pl.when(j > 0)
-            def _():
-                arrived(slot)
-
-            @pl.when(j == 1)
-            def _():
-                on_same.start()
-
-            for k, d in enumerate((a, b)):
-
-                @pl.when((j == 3) & (d < place))
-                def _():
-                    before_on[k].start()
-
-                @pl.when((j == 4) & (d > place))
-                def _():
-                    after_on[k].start()
+            @pl.when(j > 5)
+            def _():
+                arrived(0, slot)
 
             keys_t[:, aligned(slot, dm.block)] = kv[slot, 0].T
             score_phase(dm, kv[slot, 0], q_t, probs, scores, tops, sums, slot, pair * 2, 2)
 
-    for g in peers:
-        do_copy(g, me, g).start()
     for g in across:
         q_copy(me, g, g).wait_recv()
         turn(q_in, q_t, g)
 
-    @pl.loop(0, w + 1)
+    @pl.loop(0, dm.slots)
     def _(j):
-        slot = early(j)
+        slot = order(j)
+
+        @pl.when(j == 5)
+        def _():
+            pass_second(1)
 
         @pl.when(exists(slot))
         def _():
             score_phase(dm, kv[slot, 0], q_t, probs, scores, tops, sums, slot, (1 - pair) * 2, 2)
 
+    combine(dm, tops, sums, factors)
     own[5].wait()
     turn(do_in, do_t, me)
     de_own.wait()
-    do_copy(me, mate, mate).wait_recv()
-    turn(do_in, do_t, mate)
-
-    @pl.loop(0, w)
-    def _(j):
-        slot = late(j)
-
-        @pl.when(exists(slot))
-        def _():
-            arrived(slot)
-
-            @pl.when(j == 0)
-            def _():
-                on_side.start()
-
-            keys_t[:, aligned(slot, dm.block)] = kv[slot, 0].T
-            score_phase(dm, kv[slot, 0], q_t, probs, scores, tops, sums, slot, 0, 4)
-
-    combine(dm, tops, sums, factors)
-    de_copy(me, mate, mate).wait_recv()
-    for g in across:
+    for g in [mate] + across:
         do_copy(me, g, g).wait_recv()
         de_copy(me, g, g).wait_recv()
         turn(do_in, do_t, g)
+    arrived(1, same(b))
+    arrived(1, same(o))
+    for d in (a, o):
+
+        @pl.when(exists(side(d)))
+        def _():
+            arrived(1, side(d))
 
     def give(slot, box, k, to):
         return remote(dkv.at[slot], inbox.at[box], s_out.at[k], r_box.at[box], blk=to)
@@ -347,16 +383,16 @@
         )
 
     def first(j):
-        return pick(j, [side(o), same(o), side(a), side(b), same(b)])
+        return pick(j, [side(o), same(o), side(a)])
 
     def last(j):
-        return pick(j, [jnp.int32(0), jnp.int32(2 * w), same(a), jnp.int32(w)])
+        return pick(j, [side(b), same(a), same(b), jnp.int32(0), jnp.int32(2 * w), jnp.int32(w)])
 
     def add(slot, box):
         taken(box)
         dkv[slot] = (dkv[slot].astype(F32) + inbox[box].astype(F32)).astype(BF)
 
-    @pl.loop(0, w + 1)
+    @pl.loop(0, 3)
     def _(j):
         slot = first(j)
 
@@ -365,14 +401,9 @@
             dk, dv = gradients(slot, 0, 4)
             dkv[slot, 0] = dk.astype(BF)
             dkv[slot, 1] = dv.astype(BF)
-
-            @pl.when(j == 3)
-            def _():
-                add(slot, 0)
-
-            give(slot, j, j, base + pick(j, [a, b, a, b, b])).start()
-
-    @pl.loop(0, w)
+            give(slot, j, j, base + pick(j, [a, b, a])).start()
+
+    @pl.loop(0, 6)
     def _(j):
         slot = last(j)
 
@@ -392,7 +423,7 @@
         turn_back(g)
         dq_copy(g, me, g).start()
 
-    @pl.loop(0, w)
+    @pl.loop(0, 6)
     def _(j):
         slot = last(j)
 
@@ -404,6 +435,20 @@
 
             @pl.when(j == 0)
             def _():
+                add(slot, 0)
+                give(slot, 3, 3, base + b).start()
+
+            @pl.when(j == 1)
+            def _():
+                add(slot, 1)
+                give(slot, 5, 5, base + a).start()
+
+            @pl.when(j == 2)
+            def _():
+                give(slot, 4, 4, base + b).start()
+
+            @pl.when(j == 3)
+            def _():
                 for box, d in ((2, a), (3, b)):
 
                     @pl.when(d < place)
@@ -412,7 +457,7 @@
 
                 give(0, 7, 6, position - w).start()
 
-            @pl.when(j == 1)
+            @pl.when(j == 4)
             def _():
                 for box, d in ((2, a), (3, b)):
 
@@ -421,11 +466,6 @@
                         add(2 * w, box)
 
                 give(2 * w, 6, 7, position + w).start()
-
-            @pl.when(j == 2)
-            def _():
-                add(same(a), 1)
-                give(same(a), 5, 5, base + a).start()
 
     turn_back(mate)
     dq_copy(mate, me, mate).start()
@@ -434,8 +474,9 @@
     dq_own.start()
 
     total[...] = dkv[w].astype(F32)
-    taken(4)
-    total[...] += inbox[4].astype(F32)
+    for box in (5, 4):
+        taken(box)
+        total[...] += inbox[box].astype(F32)
 
     @pl.when(has_before)
     def _():
@@ -447,8 +488,6 @@
         taken(7)
         total[...] += inbox[7].astype(F32)
 
-    taken(5)
-    total[...] += inbox[5].astype(F32)
     for part in range(2):
         rows = total[part].T.astype(BF)
         for g in range(n):
@@ -471,36 +510,20 @@
 
     dq_own.wait()
     for g in peers:
-        for make in (kv_copy, q_copy, do_copy, de_copy, dq_copy, head_copy):
+        for make in (k_copy, v_copy, q_copy, do_copy, de_copy, dq_copy, head_copy):
             make(g, me, g).wait_send()
         dq_copy(me, g, g).wait_recv()
-    to_a.wait_send()
-    to_b.wait_send()
-    on_same.wait_send()
+    for part in range(2):
+        for group in (from_own, from_first, from_second):
+            group(part, lambda copy: copy.wait_send())
 
     @pl.when(has_before)
     def _():
-        to_before.wait_send()
         give(0, 7, 6, position - w).wait_send()
 
     @pl.when(has_after)
     def _():
-        to_after.wait_send()
         give(2 * w, 6, 7, position + w).wait_send()
-
-    for k, d in enumerate((a, b)):
-
-        @pl.when((d < place) & has_before)
-        def _():
-            before_on[k].wait_send()
-
-        @pl.when((d > place) & has_after)
-        def _():
-            after_on[k].wait_send()
-
-    @pl.when(exists(side(b)))
-    def _():
-        on_side.wait_send()
 
     for j in range(w + 1):
         slot = [side(o), same(o), side(a), side(b), same(b)][j]
@@ -555,10 +578,11 @@
             pltpu.VMEM((n, 2, dm.tokens, dm.width), BF),
             pltpu.VMEM((n, 2, dm.tokens, dm.width), BF),
             pltpu.VMEM(chunked, BF),
-            dma((10,)),
+            dma((11,)),
         ]
-        + [dma((n,))] * 12
-        + [dma((4,)), dma((4,)), dma((dm.slots,)), dma((8,)), dma((8,))],
+        + [dma((2, n))] * 2
+        + [dma((n,))] * 10
+        + [dma((2, 8)), dma((2, dm.slots)), dma((8,)), dma((8,))],
         compiler_params=pltpu.CompilerParams(
             collective_id=0, has_side_effects=True, vmem_limit_bytes=63 * 2**20
         ),

time: 109 us -> 109 us (level)
  no operation moved by 1% of the time
where the time goes in v2:
time: 109 us
  Pallas kernels  105 us (96%)
  local copies, waits for them, and re-layouts  3.91 us (4%)
    pallas_call x1, Pallas kernels, fused(): pl.pallas_call(functools.partial(kernel, dm), out_shape=(jax.ShapeDtypeSt...  105 us
    unnamed x7, local copies, waits for them, and re-layouts  3.91 us

profile of v2, /device:TPU:5, one launch (start us, length us, event | category | flops | bytes accessed | tf_op | source)
XLA Modules:
  0.0 109.1 jit_solution(4450327510102236524)
XLA Ops:
  0.6 104.6 %banded_attention_gradients.1 = (bf16[128,32,128]{2,1,0:T(8,128)(2,1)}, bf16[512,128]{1,0:T(8,128)(2,1)}, bf16[512,128]{1,0:T(8,128)(2,1)}) custom-call(bf16[128,32,128]{2,1,0:T(8,128)(2,1)} %query.1, bf16[128,32,128]{2,1,0:T(8,128)(2,1)} %dout.1, bf16[128,32,128]{2,1,0:T(8,128)(2,1)} %output.1, bf16[512,128]{1,0:T(8,128)(2,1)} %bitcast.6, ...), custom_call_target="tpu_custom_call" | custom-call | tf_op jit(solution)/shard_map/banded_attention_gradients/pallas_call | solution.py:544
  105.2 0.0 copy-start.1
  105.2 2.3 %copy.11 = bf16[128,32,128]{2,1,0:T(8,128)(2,1)} copy(bf16[128,32,128]{2,1,0:T(8,128)(2,1)} %get-tuple-element.12) | data formatting | bytes 2097152
  107.5 0.0 copy-done.1
  107.5 0.0 copy-start
  107.5 0.7 copy.12
  108.2 0.3 copy-done
  108.5 0.7 copy.13
Async XLA Ops:
  105.2 2.3 %copy-start.1 = (bf16[512,128]{1,0:T(8,128)(2,1)S(1)}, bf16[512,128]{1,0:T(8,128)(2,1)}, u32[]{:S(2)}) copy-start(bf16[512,128]{1,0:T(8,128)(2,1)} %get-tuple-element.7) | copy-start | bytes 393220
  107.5 1.0 copy-start

commit v3 on v2

--- a/solution.py
+++ b/solution.py
@@ -214,8 +214,7 @@
         k_copy(g, me, g).start()
     k_own = pltpu.make_async_copy(staged.at[me, 0], kv.at[w, 0, aligned(me, dm.tokens), :], local.at[6])
     k_own.start()
-    for g in peers:
-        q_copy(g, me, g).start()
+    q_copy(mate, me, mate).start()
     own[1].wait()
     split_heads(dm, values_v, staged, wide, 1)
     for g in peers:
@@ -288,6 +287,8 @@
         from_second(part, lambda copy: copy.start())
 
     from_own(0, lambda copy: copy.start())
+    for g in across:
+        q_copy(g, me, g).start()
     own[2].wait()
     own[3].wait()
     delta_rows(dm, dout_v, output_v, drow)
@@ -322,8 +323,6 @@
         @pl.when(j == 5)
         def _():
             pass_second(0)
-            for g in peers:
-                do_copy(g, me, g).start()
 
         @pl.when(j == 7)
         def _():
@@ -340,6 +339,9 @@
 
     for g in across:
         q_copy(me, g, g).wait_recv()
+    for g in across + [mate]:
+        do_copy(g, me, g).start()
+    for g in across:
         turn(q_in, q_t, g)
 
     @pl.loop(0, dm.slots)

time: 109 us -> 104 us (0.954)
  Pallas kernels: 105 us -> 98.9 us
    pallas_call x1, Pallas kernels: 105 us -> 98.9 us  [fused(): pl.pallas_call(functools.partial(kernel, dm), out_shape=(jax.ShapeDtypeSt...]
where the time goes in v3:
time: 104 us; the launch traced here: 103 us
  Pallas kernels  98.9 us (95%)
  local copies, waits for them, and re-layouts  3.91 us (4%)
    pallas_call x1, Pallas kernels, fused(): pl.pallas_call(functools.partial(kernel, dm), out_shape=(jax.ShapeDtypeSt...  98.9 us
    unnamed x7, local copies, waits for them, and re-layouts  3.91 us

profile of v3, /device:TPU:5, one launch (start us, length us, event | category | flops | bytes accessed | tf_op | source)
XLA Modules:
  0.0 103.5 jit_solution(15415154883166981611)
XLA Ops:
  0.6 98.9 %banded_attention_gradients.1 = (bf16[128,32,128]{2,1,0:T(8,128)(2,1)}, bf16[512,128]{1,0:T(8,128)(2,1)}, bf16[512,128]{1,0:T(8,128)(2,1)}) custom-call(bf16[128,32,128]{2,1,0:T(8,128)(2,1)} %query.1, bf16[128,32,128]{2,1,0:T(8,128)(2,1)} %dout.1, bf16[128,32,128]{2,1,0:T(8,128)(2,1)} %output.1, bf16[512,128]{1,0:T(8,128)(2,1)} %bitcast.6, ...), custom_call_target="tpu_custom_call" | custom-call | tf_op jit(solution)/shard_map/banded_attention_gradients/pallas_call | solution.py:546
  99.6 0.0 copy-start.1
  99.6 2.3 %copy.11 = bf16[128,32,128]{2,1,0:T(8,128)(2,1)} copy(bf16[128,32,128]{2,1,0:T(8,128)(2,1)} %get-tuple-element.12) | data formatting | bytes 2097152
  101.9 0.0 copy-done.1
  101.9 0.0 copy-start
  101.9 0.7 copy.12
  102.5 0.3 copy-done
  102.8 0.7 copy.13
Async XLA Ops:
  99.6 2.3 %copy-start.1 = (bf16[512,128]{1,0:T(8,128)(2,1)S(1)}, bf16[512,128]{1,0:T(8,128)(2,1)}, u32[]{:S(2)}) copy-start(bf16[512,128]{1,0:T(8,128)(2,1)} %get-tuple-element.7) | copy-start | bytes 393220
  101.9 1.0 copy-start

commit v4 on v3

--- a/solution.py
+++ b/solution.py
@@ -30,7 +30,7 @@
         self.rows = self.chunk * self.n_head
         self.scaling = self.width ** (-0.5)
         self.log2_scaling = self.scaling * math.log2(math.e)
-        self.score_tile = 512
+        self.score_tile = 256
         self.grad_tile = 256
 
 
@@ -73,19 +73,24 @@
     block, tile = dm.block, dm.score_tile
     count = count * dm.chunk // tile
     start = chunk * (dm.chunk // tile)
+    step = 32
+    top = None
     for i in range(count + 1):
+        before = top
         if i < count:
             columns = aligned(start + i, tile)
-            scores[i % 2] = jnp.dot(keys, q_t[:, columns], preferred_element_type=F32)
+            x = jnp.dot(keys, q_t[:, columns], preferred_element_type=F32)
+            scores[i % 2] = x
+            top = jnp.max(jnp.max(x.reshape(block // 8, 8, tile), axis=0), axis=0, keepdims=True)
         if i > 0:
             columns = aligned(start + i - 1, tile)
-            x = scores[(i - 1) % 2]
-            top = jnp.max(jnp.max(x.reshape(block // 8, 8, tile), axis=0), axis=0, keepdims=True)
-            p = jnp.exp2((x - top) * dm.log2_scaling)
-            total = jnp.sum(jnp.sum(p.reshape(block // 8, 8, tile), axis=0), axis=0, keepdims=True)
-            probs[aligned(b, block), columns] = p.astype(BF)
-            tops[pl.ds(b, 1), columns] = top
-            sums[pl.ds(b, 1), columns] = total
+            total = jnp.zeros((8, tile), F32)
+            for at in range(0, block, step):
+                p = jnp.exp2((scores[(i - 1) % 2, at:at + step] - before) * dm.log2_scaling)
+                total = total + jnp.sum(p.reshape(step // 8, 8, tile), axis=0)
+                probs[aligned(b * (block // step) + at // step, step), columns] = p.astype(BF)
+            tops[pl.ds(b, 1), columns] = before
+            sums[pl.ds(b, 1), columns] = jnp.sum(total, axis=0, keepdims=True)
 
 
 def combine(dm, tops, sums, factors):
@@ -324,10 +329,6 @@
         def _():
             pass_second(0)
 
-        @pl.when(j == 7)
-        def _():
-            pass_first(1)
-
         @pl.when(exists(slot))
         def _():
             @pl.when(j > 5)
@@ -341,6 +342,7 @@
         q_copy(me, g, g).wait_recv()
     for g in across + [mate]:
         do_copy(g, me, g).start()
+    pass_first(1)
     for g in across:
         turn(q_in, q_t, g)
 
@@ -348,7 +350,7 @@
     def _(j):
         slot = order(j)
 
-        @pl.when(j == 5)
+        @pl.when(j == 6)
         def _():
             pass_second(1)
 

time: 104 us -> 98.5 us (0.947)
  Pallas kernels: 98.9 us -> 93.1 us
    pallas_call x1, Pallas kernels: 98.9 us -> 93.1 us  [fused(): pl.pallas_call(functools.partial(kernel, dm), out_shape=(jax.ShapeDtypeSt...]
where the time goes in v4:
time: 98.5 us; the launch traced here: 97.7 us
  Pallas kernels  93.1 us (95%)
  local copies, waits for them, and re-layouts  3.91 us (4%)
    pallas_call x1, Pallas kernels, fused(): pl.pallas_call(functools.partial(kernel, dm), out_shape=(jax.ShapeDtypeSt...  93.1 us
    unnamed x7, local copies, waits for them, and re-layouts  3.91 us

profile of v4, /device:TPU:5, one launch (start us, length us, event | category | flops | bytes accessed | tf_op | source)
XLA Modules:
  0.0 97.7 jit_solution(13261051019822637369)
XLA Ops:
  0.6 93.1 %banded_attention_gradients.1 = (bf16[128,32,128]{2,1,0:T(8,128)(2,1)}, bf16[512,128]{1,0:T(8,128)(2,1)}, bf16[512,128]{1,0:T(8,128)(2,1)}) custom-call(bf16[128,32,128]{2,1,0:T(8,128)(2,1)} %query.1, bf16[128,32,128]{2,1,0:T(8,128)(2,1)} %dout.1, bf16[128,32,128]{2,1,0:T(8,128)(2,1)} %output.1, bf16[512,128]{1,0:T(8,128)(2,1)} %bitcast.6, ...), custom_call_target="tpu_custom_call" | custom-call | tf_op jit(solution)/shard_map/banded_attention_gradients/pallas_call | solution.py:548
  93.8 0.0 copy-start.1
  93.8 2.3 %copy.11 = bf16[128,32,128]{2,1,0:T(8,128)(2,1)} copy(bf16[128,32,128]{2,1,0:T(8,128)(2,1)} %get-tuple-element.12) | data formatting | bytes 2097152
  96.1 0.0 copy-done.1
  96.1 0.0 copy-start
  96.1 0.7 copy.12
  96.7 0.3 copy-done
  97.0 0.7 copy.13
Async XLA Ops:
  93.8 2.3 %copy-start.1 = (bf16[512,128]{1,0:T(8,128)(2,1)S(1)}, bf16[512,128]{1,0:T(8,128)(2,1)}, u32[]{:S(2)}) copy-start(bf16[512,128]{1,0:T(8,128)(2,1)} %get-tuple-element.7) | copy-start | bytes 393220
  96.1 1.0 copy-start

commit v5 on v4

--- a/solution.py
+++ b/solution.py
@@ -319,7 +319,6 @@
         @pl.when(j == 1)
         def _():
             pass_first(0)
-            arrived(0, same(b))
             v_own.wait()
             for g in peers:
                 v_copy(me, g, g).wait_recv()
@@ -331,7 +330,7 @@
 
         @pl.when(exists(slot))
         def _():
-            @pl.when(j > 5)
+            @pl.when((j > 5) | (j == 2))
             def _():
                 arrived(0, slot)
 

time: 98.5 us -> 98.5 us (level)
  no operation moved by 1% of the time
where the time goes in v5:
time: 98.5 us; the launch traced here: 97.7 us
  Pallas kernels  93.1 us (95%)
  local copies, waits for them, and re-layouts  3.91 us (4%)
    pallas_call x1, Pallas kernels, fused(): pl.pallas_call(functools.partial(kernel, dm), out_shape=(jax.ShapeDtypeSt...  93.1 us
    unnamed x7, local copies, waits for them, and re-layouts  3.91 us

profile of v5, /device:TPU:5, one launch (start us, length us, event | category | flops | bytes accessed | tf_op | source)
XLA Modules:
  0.0 97.7 jit_solution(14875654025622738959)
XLA Ops:
  0.6 93.1 %banded_attention_gradients.1 = (bf16[128,32,128]{2,1,0:T(8,128)(2,1)}, bf16[512,128]{1,0:T(8,128)(2,1)}, bf16[512,128]{1,0:T(8,128)(2,1)}) custom-call(bf16[128,32,128]{2,1,0:T(8,128)(2,1)} %query.1, bf16[128,32,128]{2,1,0:T(8,128)(2,1)} %dout.1, bf16[128,32,128]{2,1,0:T(8,128)(2,1)} %output.1, bf16[512,128]{1,0:T(8,128)(2,1)} %bitcast.6, ...), custom_call_target="tpu_custom_call" | custom-call | tf_op jit(solution)/shard_map/banded_attention_gradients/pallas_call | solution.py:547
  93.8 0.0 copy-start.1
  93.8 2.3 %copy.11 = bf16[128,32,128]{2,1,0:T(8,128)(2,1)} copy(bf16[128,32,128]{2,1,0:T(8,128)(2,1)} %get-tuple-element.12) | data formatting | bytes 2097152
  96.1 0.0 copy-done.1
  96.1 0.0 copy-start
  96.1 0.7 copy.12
  96.7 0.3 copy-done
  97.0 0.7 copy.13
Async XLA Ops:
  93.8 2.3 %copy-start.1 = (bf16[512,128]{1,0:T(8,128)(2,1)S(1)}, bf16[512,128]{1,0:T(8,128)(2,1)}, u32[]{:S(2)}) copy-start(bf16[512,128]{1,0:T(8,128)(2,1)} %get-tuple-element.7) | copy-start | bytes 393220
  96.1 1.0 copy-start
